TPU v7x, 32 devices: a whole 2x2x4 slice. The times are simulated.
32 devices in a mesh: pair: 4 (over y, core), rows: 8 (over z, x).
Axes of the slice: x: 2, y: 2, z: 4, core: 2. Of those that a mesh axis runs over, the one named last changes fastest.
Arguments:
- snapshot: float32 [1536, 2048], P('rows', 'pair'), may hold values from -40 to 40
- keep_side: int32 [2, 4], P(None, 'pair'), may hold values 0 or 1
Outputs:
- rotated: float32 [1536, 2048], P('rows', 'pair')
All inputs are finite; a program needn't handle non-finite values. No bound on the sum of `keep_side` on one device may be relied on, other than what follows from the above.
Results may differ from a plain program's by a relative error of at most 0.00013.
Values sent between devices are 32-bit elements; how exact they have to be, the bound alone decides.
A program may use at most 64 MiB of HBM per device.

v0:
```python
import jax
import jax.numpy as jnp
from jax import lax
from jax.sharding import PartitionSpec as P

ROUNDS = 2


EPS = 1e-06


def shifted(value, axis, steps):
    count = lax.axis_size(axis)
    pairs = [(source, (source + steps) % count) for source in range(count)]
    return lax.ppermute(value, axis, pairs)


def polar_map(gram, total_rows):
    high = lax.Precision.HIGHEST
    width = gram.shape[0]
    diag_vals = jnp.diagonal(gram)
    inv_norm = lax.rsqrt(diag_vals / total_rows + EPS)
    corr = gram * inv_norm[:, None] * inv_norm[None, :] / total_rows
    scale = jnp.sqrt(jnp.sum(corr * corr) / width)
    e_mat = corr / scale
    eye = jnp.eye(width, dtype=jnp.float32)
    e_two = jnp.dot(e_mat, e_mat, precision=high)
    b_one = (9.0 * e_mat - 6.0 * e_two + jnp.dot(e_mat, e_two, precision=high)) * 0.25
    t_zero = (3.0 * eye - e_mat) * 0.5
    t_one = (3.0 * eye - b_one) * 0.5
    z_two = jnp.dot(t_zero, t_one, precision=high)
    b_two = jnp.dot(jnp.dot(b_one, t_one, precision=high), t_one, precision=high)
    t_two = (3.0 * eye - b_two) * 0.5
    z_three = jnp.dot(z_two, t_two, precision=high)
    return z_three * (inv_norm / jnp.sqrt(scale))[:, None]


def assemble(upper_left, corner, lower_right):
    upper = jnp.concatenate([upper_left, corner], axis=1)
    lower = jnp.concatenate([corner.T, lower_right], axis=1)
    return jnp.concatenate([upper, lower], axis=0)


def full_gram(block):
    high = lax.Precision.HIGHEST
    half = block.shape[1] // 2
    left = block[:, :half]
    right = block[:, half:]
    upper_left, corner, lower_right = lax.psum(
        (
            jnp.dot(left.T, left, precision=high),
            jnp.dot(left.T, right, precision=high),
            jnp.dot(right.T, right, precision=high),
        ),
        "rows",
    )
    return assemble(upper_left, corner, lower_right)


def local(snapshot, keep_side):
    high = lax.Precision.HIGHEST
    block = snapshot
    total_rows = block.shape[0] * lax.axis_size("rows")
    half = block.shape[1] // 2
    for turn in range(ROUNDS):
        gram = full_gram(block)
        rotation = polar_map(gram, total_rows)
        block = jnp.dot(block, rotation, precision=high)
        first = block[:, :half]
        second = block[:, half:]
        chosen = keep_side[turn, 0]
        forward = jnp.where(chosen == 0, first, second)
        backward = jnp.where(chosen == 0, second, first)
        arrived_fwd = shifted(forward, "pair", 1)
        arrived_bwd = shifted(backward, "pair", -1)
        block = jnp.concatenate([arrived_fwd, arrived_bwd], axis=1)
    return block


def solution(mesh):
    placed = (P("rows", "pair"), P(None, "pair"))
    return jax.shard_map(
        local, mesh=mesh, in_specs=placed, out_specs=P("rows", "pair"), check_vma=False
    )
```

profile of v0, /device:TPU:1, one launch (start us, length us, event | category | flops | bytes accessed | tf_op | source)
XLA Modules:
  0.0 233.5 jit_solution(4328980385168516040)
XLA Ops:
  6.5 2.4 %fusion.44 = f32[256,256]{1,0:T(8,128)} fusion(f32[192,512]{1,0:T(8,128)} %param.2), kind=kOutput, calls=%fused_computation.62 | convolution fusion | flops 150994944 | bytes 458752 | tf_op jit(solution)/shard_map/dot_general | solution.py:53
  9.0 1.4 fusion.49
  10.4 1.4 fusion.46
  13.6 74.7 %all-reduce.7.cloned.1.call-done = (f32[256,256]{1,0:T(8,128)}, f32[256,256]{0,1:T(8,128)}, f32[256,256]{1,0:T(8,128)}) async-done(((f32[256,256]{1,0:T(8,128)}, f32[256,256]{0,1:T(8,128)}, f32[256,256]{1,0:T(8,128)}), (f32[256,256]{1,0:T(8,128)}, f32[256,256]{0,1:T(8,128)}, f32[256,256]{1,0:T(8,128)})) %all-reduce.7.cloned.1.call-update) | async-done | bytes 786448 | tf_op jit(solution)/shard_map/psum | solution.py:49
  88.3 1.1 copy.9
  89.5 1.1 maximum_maximum_fusion
  90.6 4.7 %gather_fusion = f32[512]{0:T(512)S(1)} fusion(f32[512,512]{1,0:T(8,128)S(1)} %maximum_maximum_fusion, s32[512]{0:T(512)S(1)} %bitcast.26), kind=kCustom, calls=%fused_computation | custom fusion | bytes 8192 | tf_op jit(solution)/shard_map/jit(diagonal)/cond/branch_0_fun/gather | solution.py:21
  97.0 2.2 fusion.74
  99.2 2.2 fusion.1
  101.4 2.1 fusion.5
  103.6 1.9 fusion.9
  105.5 1.9 fusion.2
  107.4 1.8 convolution_multiply_fusion.1
  109.3 1.2 convolution_bitcast_fusion
  110.5 2.0 collective-permute-start.1
  112.5 1.1 collective-permute-start
  113.6 5.6 %collective-permute-done.1 = f32[192,256]{1,0:T(8,128)S(1)} collective-permute-done((f32[192,256]{1,0:T(8,128)S(1)}, f32[192,256]{1,0:T(8,128)S(1)}, u32[]{:S(2)}, u32[]{:S(2)}) %collective-permute-start.1) | collective-permute-done | bytes 196640 | tf_op jit(solution)/shard_map/ppermute | solution.py:15
  119.3 1.4 fusion.81
  120.7 1.4 fusion.80
  122.1 1.4 fusion.79
  124.1 71.6 %all-reduce.5.cloned.1.call-done = (f32[256,256]{1,0:T(8,128)}, f32[256,256]{0,1:T(8,128)}, f32[256,256]{0,1:T(8,128)}) async-done(((f32[256,256]{1,0:T(8,128)}, f32[256,256]{0,1:T(8,128)}, f32[256,256]{0,1:T(8,128)}), (f32[256,256]{1,0:T(8,128)}, f32[256,256]{0,1:T(8,128)}, f32[256,256]{0,1:T(8,128)})) %all-reduce.5.cloned.1.call-update) | async-done | bytes 786448 | tf_op jit(solution)/shard_map/psum | solution.py:49
  195.7 1.1 pad_maximum_fusion
  197.9 4.5 %gather_fusion.1 = f32[512]{0:T(512)S(1)} fusion(f32[512,512]{1,0:T(8,128)S(1)} %maximum_maximum_fusion.1, s32[512]{0:T(512)S(1)} %bitcast.27), kind=kCustom, calls=%fused_computation.1 | custom fusion | bytes 8192 | tf_op jit(solution)/shard_map/jit(diagonal)/cond/branch_0_fun/gather | solution.py:21
  204.2 2.2 fusion.70
  206.4 2.2 fusion
  208.5 2.1 fusion.13
  210.7 1.9 fusion.17
  212.6 1.9 fusion.3
  214.5 1.9 convolution_multiply_fusion
  217.3 3.1 %collective-permute-start.2 = (f32[192,256]{1,0:T(8,128)S(1)}, f32[192,256]{1,0:T(8,128)S(1)}, u32[]{:S(2)}, u32[]{:S(2)}) collective-permute-start(f32[192,256]{1,0:T(8,128)S(1)} %get-tuple-element.11), channel_id=1, source_target_pairs={{0,8},{8,16},{16,24},{24,0},{1,9},{9,17},{17,25},{25,1},{2,10},{10... | collective-permute-start | bytes 589832 | tf_op jit(solution)/shard_map/ppermute | solution.py:15
  220.4 3.9 %collective-permute-done.2 = f32[192,256]{1,0:T(8,128)S(1)} collective-permute-done((f32[192,256]{1,0:T(8,128)S(1)}, f32[192,256]{1,0:T(8,128)S(1)}, u32[]{:S(2)}, u32[]{:S(2)}) %collective-permute-start.2) | collective-permute-done | bytes 196640 | tf_op jit(solution)/shard_map/ppermute | solution.py:15
  224.3 1.6 collective-permute-done.3
  (34 shorter events, 6.1 us)
Async XLA Ops:
  6.5 2.4 %copy-start = (f32[192,512]{1,0:T(8,128)S(1)}, f32[192,512]{1,0:T(8,128)}, u32[]{:S(2)}) copy-start(f32[192,512]{1,0:T(8,128)} %param.2) | copy-start | bytes 1179652
  6.5 81.8 %all-reduce.7.cloned.1.call-start = ((), (), s32[]{:S(2)}) async-start(), calls=%async_computation.1 | async-start | bytes 1572864 | tf_op jit(solution)/shard_map/psum | solution.py:49
  11.8 0.7 copy-start.6
  11.8 183.9 %all-reduce.5.cloned.1.call-start = ((), (), s32[]{:S(2)}) async-start(), calls=%async_computation | async-start | bytes 1572864 | tf_op jit(solution)/shard_map/psum | solution.py:49
  88.3 1.2 copy-start.1
  88.3 1.2 copy-start.3
  90.6 4.7 %copy-start.4 = (f32[256,256]{1,0:T(8,128)S(1)}, f32[256,256]{1,0:T(8,128)}, u32[]{:S(2)}) copy-start(f32[256,256]{1,0:T(8,128)} %get-tuple-element.10) | copy-start | bytes 786436
  110.5 8.8 %collective-permute-start.1 = (f32[192,256]{1,0:T(8,128)S(1)}, f32[192,256]{1,0:T(8,128)S(1)}, u32[]{:S(2)}, u32[]{:S(2)}) collective-permute-start(f32[192,256]{1,0:T(8,128)S(1)} %get-tuple-element.14), channel_id=1, source_target_pairs={{0,24},{8,0},{16,8},{24,16},{1,25},{9,1},{17,9},{25,17},{2,26},{10... | collective-permute-start | bytes 589832 | tf_op jit(solution)/shard_map/ppermute | solution.py:15
  112.5 8.2 %collective-permute-start = (f32[192,256]{1,0:T(8,128)S(1)}, f32[192,256]{1,0:T(8,128)S(1)}, u32[]{:S(2)}, u32[]{:S(2)}) collective-permute-start(f32[192,256]{1,0:T(8,128)S(1)} %get-tuple-element.13), channel_id=1, source_target_pairs={{0,8},{8,16},{16,24},{24,0},{1,9},{9,17},{17,25},{25,1},{2,10},{10... | collective-permute-start | bytes 589832 | tf_op jit(solution)/shard_map/ppermute | solution.py:15
  196.7 1.0 copy-start.2
  196.8 1.0 copy-start.5
  217.3 7.0 %collective-permute-start.2 = (f32[192,256]{1,0:T(8,128)S(1)}, f32[192,256]{1,0:T(8,128)S(1)}, u32[]{:S(2)}, u32[]{:S(2)}) collective-permute-start(f32[192,256]{1,0:T(8,128)S(1)} %get-tuple-element.11), channel_id=1, source_target_pairs={{0,8},{8,16},{16,24},{24,0},{1,9},{9,17},{17,25},{25,1},{2,10},{10... | collective-permute-start | bytes 589832 | tf_op jit(solution)/shard_map/ppermute | solution.py:15
  220.4 5.4 %collective-permute-start.3 = (f32[192,256]{1,0:T(8,128)S(1)}, f32[192,256]{1,0:T(8,128)S(1)}, u32[]{:S(2)}, u32[]{:S(2)}) collective-permute-start(f32[192,256]{1,0:T(8,128)S(1)} %get-tuple-element.12), channel_id=1, source_target_pairs={{0,24},{8,0},{16,8},{24,16},{1,25},{9,1},{17,9},{25,17},{2,26},{10... | collective-permute-start | bytes 589832 | tf_op jit(solution)/shard_map/ppermute | solution.py:15
Sparse Core Ops, SparseCore 0:
  11.9 76.3 all-reduce.6
  123.6 72.0 all-reduce.4
where the time goes:
time: 234 us; the launch traced here: 233 us
  waiting for transfers between devices  157 us (67%)
  matrix products  35.7 us (15%)
  between operations  16.3 us (7%)
  local copies, waits for them, and re-layouts  12.6 us (5%)
  starting transfers between devices  6.32 us (3%)
  other arithmetic  5.13 us (2%)
    psum x2, waiting for transfers between devices, full_gram(): lax.psum((jnp.dot(left.T, left, precision=high), jnp.dot(left.T, right, p...  146 us
    ppermute x4, waiting for transfers between devices, shifted(): return lax.ppermute(value, axis, pairs)  11.1 us
    gather x2, local copies, waits for them, and re-layouts, polar_map(): diag_vals = jnp.diagonal(gram)  9.23 us
    ppermute x4, starting transfers between devices, shifted(): return lax.ppermute(value, axis, pairs)  6.28 us
  transfers between devices with their start and end apart: 6, of which 5 were waited for; matrix products, arithmetic and copies ran while one was open for 1% of the time, Pallas kernels for 0%

commit v1 on v0

v1 whole, which is shorter than its diff:
```python
import functools

import jax
import jax.numpy as jnp
from jax import lax
from jax.experimental import pallas as pl
from jax.experimental.pallas import tpu as pltpu
from jax.sharding import PartitionSpec as P

ROUNDS = 2
EPS = 1e-06
TILE = 128
MESH = pl.DeviceIdType.MESH
F32 = jnp.float32
BF16 = jnp.bfloat16


def split(value):
    high = value.astype(BF16)
    low = (value - high.astype(F32)).astype(BF16)
    return high, low


def dot(a, b):
    return jnp.dot(a, b, preferred_element_type=F32)


def dot_split(a, b):
    rows = a[0].shape[0]
    both = dot(jnp.concatenate([a[0], a[1]], axis=0), b[0])
    return both[:rows] + both[rows:] + dot(a[0], b[1])


def tiles_of(width):
    count = width // TILE
    return [(i, j) for i in range(count) for j in range(i, count)]


def local_gram(left, right, acc):
    high, low = split(jnp.concatenate([left, right], axis=1))
    lhs = jnp.concatenate([high, high, low], axis=0).T
    rhs = jnp.concatenate([high, low, high], axis=0)
    width = rhs.shape[1]
    place = 0
    for i in range(width // TILE):
        strip = dot(lhs[i * TILE:(i + 1) * TILE], rhs[:, i * TILE:])
        for j in range(width // TILE - i):
            acc[place * TILE:(place + 1) * TILE, :] = strip[:, j * TILE:(j + 1) * TILE]
            place += 1


def all_reduce(n_rows, masks, acc, full, rbuf, send_sem, recv_sem):
    me = lax.axis_index("rows")
    parts = len(masks)
    steps = len(masks[0])
    length = acc.shape[0] // parts
    copies = []

    def bit(mask):
        return lax.rem(me // mask, 2)

    def peer(mask):
        return me + mask * (1 - 2 * bit(mask))

    def remote(src, dst, slot, mask):
        copy = pltpu.make_async_remote_copy(
            src_ref=src, dst_ref=dst, send_sem=send_sem.at[slot], recv_sem=recv_sem.at[slot],
            device_id={"rows": peer(mask)}, device_id_type=MESH)
        copy.start()
        copies.append(copy)
        return copy

    keep = [[part * length] for part in range(parts)]
    pending = [None] * parts
    for k in range(steps + 1):
        half = length >> (k + 1)
        for part in range(parts):
            base = part * length
            here = keep[part][-1]
            if k > 0:
                pending[part].wait_recv()
                got = rbuf[pl.ds(base + length - 2 * (length >> k), length >> k), :]
                span = pl.ds(pl.multiple_of(here, 8), length >> k)
                if k == steps:
                    full[span, :] = acc[span, :] + got
                else:
                    acc[span, :] = acc[span, :] + got
            if k < steps:
                mask = masks[part][k]
                own = bit(mask)
                keep[part].append(here + own * half)
                away = pl.multiple_of(here + (1 - own) * half, 8)
                pending[part] = remote(
                    acc.at[pl.ds(away, half), :],
                    rbuf.at[pl.ds(base + length - 2 * half, half), :],
                    part * 2 * steps + k, mask)
    for k in reversed(range(steps)):
        half = length >> (k + 1)
        for part in range(parts):
            if k < steps - 1:
                pending[part].wait_recv()
            span = pl.ds(pl.multiple_of(keep[part][k + 1], 8), half)
            pending[part] = remote(
                full.at[span, :], full.at[span, :], part * 2 * steps + steps + k, masks[part][k])
    for part in range(parts):
        pending[part].wait_recv()
    return copies


def rotate(left, right, full, total_rows):
    block = jnp.concatenate([left, right], axis=1)
    width = block.shape[1]
    count = width // TILE
    at = {pair: full[n * TILE:(n + 1) * TILE, :] for n, pair in enumerate(tiles_of(width))}
    unit = (lax.broadcasted_iota(jnp.int32, (TILE, TILE), 0)
            == lax.broadcasted_iota(jnp.int32, (TILE, TILE), 1))
    diag = [jnp.where(unit, at[i, i], 0.0) for i in range(count)]
    as_row = [lax.rsqrt(jnp.sum(d, axis=0, keepdims=True) / total_rows + EPS) for d in diag]
    as_col = [lax.rsqrt(jnp.sum(d, axis=1, keepdims=True) / total_rows + EPS) for d in diag]
    energy = jnp.zeros((1, TILE), F32)
    for i, j in tiles_of(width):
        at[i, j] = at[i, j] * as_col[i] * as_row[j] / total_rows
        part = jnp.sum(at[i, j] * at[i, j], axis=0, keepdims=True)
        energy = energy + (part if i == j else 2.0 * part)
    scale = jnp.sqrt(jnp.sum(energy, axis=1, keepdims=True) / width)
    inv_scale = 1.0 / scale
    for i, j in tiles_of(width):
        at[i, j] = at[i, j] * inv_scale
        if i != j:
            at[j, i] = at[i, j].T
    e_mat = jnp.concatenate(
        [jnp.concatenate([at[i, j] for j in range(count)], axis=1) for i in range(count)], axis=0)
    e_half = split(e_mat)
    e_two = dot_split(e_half, e_half)
    e_three = dot_split(e_half, split(e_two))
    wide = (lax.broadcasted_iota(jnp.int32, (width, width), 0)
            == lax.broadcasted_iota(jnp.int32, (width, width), 1))
    b_one = (9.0 * e_mat - 6.0 * e_two + e_three) * 0.25
    t_half = split(jnp.where(wide, 1.5, 0.0) - 0.5 * b_one)
    inv_norm = jnp.concatenate(as_row, axis=1) * lax.rsqrt(scale)
    y = block * inv_norm
    y = 1.5 * y - 0.5 * dot_split(split(y), e_half)
    y = dot_split(split(y), t_half)
    b = 3.0 * y - 2.0 * dot_split(split(y), t_half)
    b = dot_split(split(b), t_half)
    b = dot_split(split(b), t_half)
    return 1.5 * y - 0.5 * b


def kernel(n_rows, n_pair, masks, side, x, out, acc, full, rbuf, leave, land,
           row_send, row_recv, pair_send, pair_recv):
    p = lax.axis_index("pair")
    r = lax.axis_index("rows")
    after = lax.rem(p + 1, n_pair)
    before = lax.rem(p + n_pair - 1, n_pair)
    barrier = pltpu.get_barrier_semaphore()
    for mask in sorted(masks[0]):
        other = r + mask * (1 - 2 * lax.rem(r // mask, 2))
        pl.semaphore_signal(barrier, inc=1, device_id={"rows": other}, device_id_type=MESH)
    for other in (after, before):
        pl.semaphore_signal(barrier, inc=1, device_id={"pair": other}, device_id_type=MESH)
    half = x.shape[1] // 2
    local_gram(x[:, :half], x[:, half:], acc.at[0])
    pl.semaphore_wait(barrier, len(masks[0]) + 2)
    waits = []
    for turn in range(ROUNDS):
        if turn == 0:
            halves = lambda: (x[:, :half], x[:, half:])
        else:
            halves = lambda: (land[turn - 1, 0], land[turn - 1, 1])
            local_gram(*halves(), acc.at[turn])
        waits += all_reduce(n_rows, masks, acc.at[turn], full.at[turn], rbuf.at[turn],
                            row_send.at[turn], row_recv.at[turn])
        y = rotate(*halves(), full.at[turn], x.shape[0] * n_rows)
        first, second = y[:, :half], y[:, half:]
        chosen = jnp.full(first.shape, side[turn, 0], jnp.int32) == 0
        leave[turn, 0] = jnp.where(chosen, first, second)
        leave[turn, 1] = jnp.where(chosen, second, first)
        sent = []
        for way, other in enumerate((after, before)):
            copy = pltpu.make_async_remote_copy(
                src_ref=leave.at[turn, way], dst_ref=land.at[turn, way],
                send_sem=pair_send.at[turn, way], recv_sem=pair_recv.at[turn, way],
                device_id={"pair": other}, device_id_type=MESH)
            copy.start()
            sent.append(copy)
        for copy in sent:
            copy.wait_recv()
        waits += sent
    out[:, :half] = land[ROUNDS - 1, 0]
    out[:, half:] = land[ROUNDS - 1, 1]
    for copy in waits:
        copy.wait_send()


def solution(mesh):
    n_rows = mesh.shape["rows"]
    n_pair = mesh.shape["pair"]
    powers = []
    while (1 << len(powers)) < n_rows:
        powers.append(1 << len(powers))
    masks = (tuple(powers), tuple(powers[1:] + powers[:1]))
    steps = len(powers)

    def local(snapshot, keep_side):
        rows, width = snapshot.shape
        gram_rows = len(tiles_of(width)) * TILE
        vmem = pl.BlockSpec(memory_space=pltpu.VMEM)
        return pl.pallas_call(
            functools.partial(kernel, n_rows, n_pair, masks),
            out_shape=jax.ShapeDtypeStruct((rows, width), F32),
            in_specs=[pl.BlockSpec(memory_space=pltpu.SMEM), vmem],
            out_specs=vmem,
            scratch_shapes=[
                pltpu.VMEM((ROUNDS, gram_rows, TILE), F32),
                pltpu.VMEM((ROUNDS, gram_rows, TILE), F32),
                pltpu.VMEM((ROUNDS, gram_rows, TILE), F32),
                pltpu.VMEM((ROUNDS, 2, rows, width // 2), F32),
                pltpu.VMEM((ROUNDS, 2, rows, width // 2), F32),
                pltpu.SemaphoreType.DMA((ROUNDS, 4 * steps)),
                pltpu.SemaphoreType.DMA((ROUNDS, 4 * steps)),
                pltpu.SemaphoreType.DMA((ROUNDS, 2)),
                pltpu.SemaphoreType.DMA((ROUNDS, 2)),
            ],
            compiler_params=pltpu.CompilerParams(
                collective_id=0, has_side_effects=True, vmem_limit_bytes=48 << 20),
        )(keep_side, snapshot)

    placed = (P("rows", "pair"), P(None, "pair"))
    return jax.shard_map(
        local, mesh=mesh, in_specs=placed, out_specs=P("rows", "pair"), check_vma=False
    )
```

time: 234 us -> 78.3 us (0.33)
  waiting for transfers between devices: 157 us -> 0 us
  Pallas kernels: 0 us -> 75.6 us
  matrix products: 35.7 us -> 0 us
  between operations: 16.3 us -> 0.01 us
  local copies, waits for them, and re-layouts: 12.6 us -> 2.48 us
  starting transfers between devices: 6.32 us -> 0 us
  other arithmetic: 5.13 us -> 0 us
    psum x2 -> x0, waiting for transfers between devices: 146 us -> none  [full_gram(): lax.psum((jnp.dot(left.T, left, precision=high), jnp.dot(left.T, right, p...]
    pallas_call x0 -> x1, Pallas kernels: none -> 75.6 us  [local(): pl.pallas_call(functools.partial(kernel, n_rows, n_pair, masks), out_shap...]
    dot_general x20 -> x0, matrix products: 35.7 us -> none  [the longest x2 4.37 us: polar_map(): e_two = jnp.dot(e_mat, e_mat, precision=high)]
    ppermute x4 -> x0, waiting for transfers between devices: 11.1 us -> none  [shifted(): return lax.ppermute(value, axis, pairs)]
    gather x2 -> x0, local copies, waits for them, and re-layouts: 9.23 us -> none  [polar_map(): diag_vals = jnp.diagonal(gram)]
    ppermute x4 -> x0, starting transfers between devices: 6.28 us -> none  [shifted(): return lax.ppermute(value, axis, pairs)]
    concatenate x5 -> x0, other arithmetic: 3.05 us -> none  [the longest x2 1.19 us: assemble(): return jnp.concatenate([upper, lower], axis=0)]
  transfers between devices with their start and end apart: 6 -> 0, of which waited for: 5 -> 0; matrix products, arithmetic and copies ran while one was open for 1% -> 0% of each run, Pallas kernels for 0% -> 0%
where the time goes in v1:
time: 78.3 us; the launch traced here: 78.1 us
  Pallas kernels  75.6 us (97%)
  local copies, waits for them, and re-layouts  2.48 us (3%)
    pallas_call x1, Pallas kernels, local(): pl.pallas_call(functools.partial(kernel, n_rows, n_pair, masks), out_shap...  75.6 us
    unnamed x4, local copies, waits for them, and re-layouts  2.48 us

profile of v1, /device:TPU:1, one launch (start us, length us, event | category | flops | bytes accessed | tf_op | source)
XLA Modules:
  0.0 78.1 jit_solution(1621557974750080487)
XLA Ops:
  0.0 0.7 copy.3.side
  0.7 0.0 copy-start
  0.7 1.0 %copy-done = f32[192,512]{1,0:T(8,128)S(1)} copy-done((f32[192,512]{1,0:T(8,128)S(1)}, f32[192,512]{1,0:T(8,128)}, u32[]{:S(2)}) %copy-start) | copy-done | bytes 393240
  1.7 75.6 %shard_map.28 = f32[192,512]{1,0:T(8,128)S(1)} custom-call(s32[2,1]{1,0:T(2,128)S(1)} %copy.3.side, f32[192,512]{1,0:T(8,128)S(1)} %copy-done), custom_call_target="tpu_custom_call" | custom-call | tf_op jit(solution)/shard_map/pallas_call | solution.py:209
  77.3 0.7 copy.5
Async XLA Ops:
  0.7 1.0 %copy-start = (f32[192,512]{1,0:T(8,128)S(1)}, f32[192,512]{1,0:T(8,128)}, u32[]{:S(2)}) copy-start(f32[192,512]{1,0:T(8,128)} %x.1) | copy-start | bytes 1179652

commit v2 on v1

v2 whole, which is shorter than its diff:
```python
import functools

import jax
import jax.numpy as jnp
from jax import lax
from jax.experimental import pallas as pl
from jax.experimental.pallas import tpu as pltpu
from jax.sharding import PartitionSpec as P

ROUNDS = 2
EPS = 1e-06
TILE = 128
PARTS = 4
FAR = (0, 2)
MESH = pl.DeviceIdType.MESH
F32 = jnp.float32
BF16 = jnp.bfloat16


def split(value):
    high = value.astype(BF16)
    low = (value - high.astype(F32)).astype(BF16)
    return high, low


def dot(a, b):
    return jnp.dot(a, b, preferred_element_type=F32)


def dot_split(a, b):
    rows = a[0].shape[0]
    both = dot(jnp.concatenate([a[0], a[1]], axis=0), b[0])
    return both[:rows] + both[rows:] + dot(a[0], b[1])


def off_diagonal(count):
    return [(i, j) for i in range(count) for j in range(i + 1, count)]


def packed_rows(width, unit):
    count = width // TILE
    body = (count * (count - 1) // 2 + count // 2) * TILE
    return -(-(body + 8 * (count // 2)) // unit) * unit


def square_index():
    return (lax.broadcasted_iota(jnp.int32, (TILE, TILE), 0),
            lax.broadcasted_iota(jnp.int32, (TILE, TILE), 1))


def gram_pieces(left, right, acc):
    high, low = split(jnp.concatenate([left, right], axis=1))
    lhs = jnp.concatenate([high, high, low], axis=0).T
    rhs = jnp.concatenate([high, low, high], axis=0)
    count = rhs.shape[1] // TILE
    row, col = square_index()
    strips = {}

    def tile(i, j):
        if i not in strips:
            strips[i] = dot(lhs[i * TILE:(i + 1) * TILE], rhs[:, i * TILE:])
        return strips[i][:, (j - i) * TILE:(j - i + 1) * TILE]

    place = 0
    for i, j in off_diagonal(count):
        yield place, tile(i, j)
        place += TILE
    tails = []
    for i in range(0, count, 2):
        later = tile(i + 1, i + 1)
        tails.append(jnp.sum(jnp.where(row == col, later, 0.0), axis=0, keepdims=True))
        yield place, jnp.where(row <= col, tile(i, i), later)
        place += TILE
    for tail in tails:
        yield place, jnp.broadcast_to(tail, (8, TILE))
        place += 8
    if place < acc.shape[0]:
        yield place, jnp.zeros((acc.shape[0] - place, TILE), F32)


def unpacked(full, count):
    row, col = square_index()
    at, place = {}, 0
    for pair in off_diagonal(count):
        at[pair] = full[place:place + TILE, :]
        place += TILE
    tail = place + count // 2 * TILE
    for i in range(0, count, 2):
        both = full[place:place + TILE, :]
        flipped = both.T
        diagonal = jnp.broadcast_to(full[tail:tail + 1, :], (TILE, TILE))
        at[i, i] = jnp.where(row <= col, both, flipped)
        at[i + 1, i + 1] = jnp.where(row > col, both, jnp.where(row == col, diagonal, flipped))
        place += TILE
        tail += 8
    return at


def all_reduce(plan, pieces, acc, full, rbuf, send_sem, recv_sem):
    me = lax.axis_index("rows")
    parts = len(plan)
    steps = len(plan[0][2])
    copies = []

    def bit(mask):
        return lax.rem(me // mask, 2)

    def remote(src, dst, slot, mask):
        copy = pltpu.make_async_remote_copy(
            src_ref=src, dst_ref=dst, send_sem=send_sem.at[slot], recv_sem=recv_sem.at[slot],
            device_id={"rows": me + mask * (1 - 2 * bit(mask))}, device_id_type=MESH)
        copy.start()
        copies.append(copy)
        return copy

    keep = [[start] for start, _, _ in plan]
    pending = [None] * parts
    slots = 2 * steps - 1
    filled = 0
    for k in range(steps + 1):
        for part, (base, length, masks) in enumerate(plan):
            if k == 0:
                while filled < base + length:
                    place, value = next(pieces)
                    acc[place:place + value.shape[0], :] = value
                    filled = place + value.shape[0]
            size = length >> min(k, steps - 1)
            here = keep[part][-1]
            span = pl.ds(pl.multiple_of(here, 8), size)
            if k > 0:
                pending[part].wait_recv()
                landed = base + (length - 2 * size if k < steps else length - size)
                total = acc[span, :] + rbuf[pl.ds(landed, size), :]
                if k == steps:
                    full[span, :] = total
                else:
                    acc[span, :] = total
            if k < steps - 1:
                half = size // 2
                own = bit(masks[k])
                keep[part].append(here + own * half)
                away = pl.multiple_of(here + (1 - own) * half, 8)
                pending[part] = remote(
                    acc.at[pl.ds(away, half), :], rbuf.at[pl.ds(base + length - size, half), :],
                    part * slots + k, masks[k])
            elif k == steps - 1:
                pending[part] = remote(
                    acc.at[span, :], rbuf.at[pl.ds(base + length - size, size), :],
                    part * slots + k, masks[k])
    for k in reversed(range(steps - 1)):
        for part, (base, length, masks) in enumerate(plan):
            if k < steps - 2:
                pending[part].wait_recv()
            span = pl.ds(pl.multiple_of(keep[part][k + 1], 8), length >> (k + 1))
            pending[part] = remote(full.at[span, :], full.at[span, :], part * slots + steps + k, masks[k])
    if steps > 1:
        for copy in pending:
            copy.wait_recv()
    return copies


def rotate(left, right, full, total_rows):
    block = jnp.concatenate([left, right], axis=1)
    width = block.shape[1]
    count = width // TILE
    at = unpacked(full, count)
    row, col = square_index()
    unit = row == col
    diag = [jnp.where(unit, at[i, i], 0.0) for i in range(count)]
    as_row = [lax.rsqrt(jnp.sum(d, axis=0, keepdims=True) / total_rows + EPS) for d in diag]
    as_col = [lax.rsqrt(jnp.sum(d, axis=1, keepdims=True) / total_rows + EPS) for d in diag]
    energy = jnp.zeros((1, TILE), F32)
    for i, j in sorted(at):
        at[i, j] = at[i, j] * as_col[i] * as_row[j] / total_rows
        part = jnp.sum(at[i, j] * at[i, j], axis=0, keepdims=True)
        energy = energy + (part if i == j else 2.0 * part)
    scale = jnp.sqrt(jnp.sum(energy, axis=1, keepdims=True) / width)
    inv_scale = 1.0 / scale
    for i, j in sorted(at):
        at[i, j] = at[i, j] * inv_scale
        if i != j:
            at[j, i] = at[i, j].T
    e_mat = jnp.concatenate(
        [jnp.concatenate([at[i, j] for j in range(count)], axis=1) for i in range(count)], axis=0)
    e_half = split(e_mat)
    e_two = dot_split(e_half, e_half)
    e_three = dot_split(e_half, split(e_two))
    wide = (lax.broadcasted_iota(jnp.int32, (width, width), 0)
            == lax.broadcasted_iota(jnp.int32, (width, width), 1))
    b_one = (9.0 * e_mat - 6.0 * e_two + e_three) * 0.25
    t_half = split(jnp.where(wide, 1.5, 0.0) - 0.5 * b_one)
    inv_norm = jnp.concatenate(as_row, axis=1) * lax.rsqrt(scale)
    y = block * inv_norm
    y = 1.5 * y - 0.5 * dot_split(split(y), e_half)
    y = dot_split(split(y), t_half)
    b = 3.0 * y - 2.0 * dot_split(split(y), t_half)
    b = dot_split(split(b), t_half)
    b = dot_split(split(b), t_half)
    return 1.5 * y - 0.5 * b


def kernel(n_rows, n_pair, plan, side, x, out, acc, full, rbuf, leave, land,
           row_send, row_recv, pair_send, pair_recv):
    p = lax.axis_index("pair")
    r = lax.axis_index("rows")
    after = lax.rem(p + 1, n_pair)
    before = lax.rem(p + n_pair - 1, n_pair)
    barrier = pltpu.get_barrier_semaphore()
    for mask in sorted(plan[0][2]):
        other = r + mask * (1 - 2 * lax.rem(r // mask, 2))
        pl.semaphore_signal(barrier, inc=1, device_id={"rows": other}, device_id_type=MESH)
    for other in (after, before):
        pl.semaphore_signal(barrier, inc=1, device_id={"pair": other}, device_id_type=MESH)
    half = x.shape[1] // 2
    pl.semaphore_wait(barrier, len(plan[0][2]) + 2)
    waits = []
    for turn in range(ROUNDS):
        if turn == 0:
            halves = lambda: (x[:, :half], x[:, half:])
        else:
            halves = lambda: (land[turn - 1, 0], land[turn - 1, 1])
        waits += all_reduce(plan, gram_pieces(*halves(), acc.at[turn]), acc.at[turn], full.at[turn], rbuf.at[turn],
                            row_send.at[turn], row_recv.at[turn])
        y = rotate(*halves(), full.at[turn], x.shape[0] * n_rows)
        first, second = y[:, :half], y[:, half:]
        chosen = jnp.full(first.shape, side[turn, 0], jnp.int32) == 0
        leave[turn, 0] = jnp.where(chosen, first, second)
        leave[turn, 1] = jnp.where(chosen, second, first)
        sent = []
        for way, other in enumerate((after, before)):
            copy = pltpu.make_async_remote_copy(
                src_ref=leave.at[turn, way], dst_ref=land.at[turn, way],
                send_sem=pair_send.at[turn, way], recv_sem=pair_recv.at[turn, way],
                device_id={"pair": other}, device_id_type=MESH)
            copy.start()
            sent.append(copy)
        for copy in sent:
            copy.wait_recv()
        waits += sent
    out[:, :half] = land[ROUNDS - 1, 0]
    out[:, half:] = land[ROUNDS - 1, 1]
    for copy in waits:
        copy.wait_send()


def make_plan(length, unit, powers):
    near_first = tuple(powers)
    far_first = tuple(powers[1:2] + powers[:1] + powers[2:])
    units = length // unit
    plan, start = [], 0
    for part in range(PARTS):
        size = (units * (part + 1) // PARTS - units * part // PARTS) * unit
        plan.append((start, size, far_first if part in FAR else near_first))
        start += size
    return tuple(plan)


def solution(mesh):
    n_rows = mesh.shape["rows"]
    n_pair = mesh.shape["pair"]
    powers = []
    while (1 << len(powers)) < n_rows:
        powers.append(1 << len(powers))
    steps = len(powers)

    def local(snapshot, keep_side):
        rows, width = snapshot.shape
        gram_rows = packed_rows(width, 4 * n_rows)
        plan = make_plan(gram_rows, 4 * n_rows, powers)
        vmem = pl.BlockSpec(memory_space=pltpu.VMEM)
        return pl.pallas_call(
            functools.partial(kernel, n_rows, n_pair, plan),
            out_shape=jax.ShapeDtypeStruct((rows, width), F32),
            in_specs=[pl.BlockSpec(memory_space=pltpu.SMEM), vmem],
            out_specs=vmem,
            scratch_shapes=[
                pltpu.VMEM((ROUNDS, gram_rows, TILE), F32),
                pltpu.VMEM((ROUNDS, gram_rows, TILE), F32),
                pltpu.VMEM((ROUNDS, gram_rows, TILE), F32),
                pltpu.VMEM((ROUNDS, 2, rows, width // 2), F32),
                pltpu.VMEM((ROUNDS, 2, rows, width // 2), F32),
                pltpu.SemaphoreType.DMA((ROUNDS, PARTS * (2 * steps - 1))),
                pltpu.SemaphoreType.DMA((ROUNDS, PARTS * (2 * steps - 1))),
                pltpu.SemaphoreType.DMA((ROUNDS, 2)),
                pltpu.SemaphoreType.DMA((ROUNDS, 2)),
            ],
            compiler_params=pltpu.CompilerParams(
                collective_id=0, has_side_effects=True, vmem_limit_bytes=48 << 20),
        )(keep_side, snapshot)

    placed = (P("rows", "pair"), P(None, "pair"))
    return jax.shard_map(
        local, mesh=mesh, in_specs=placed, out_specs=P("rows", "pair"), check_vma=False
    )
```

time: 78.3 us -> 66.7 us (0.85)
  Pallas kernels: 75.6 us -> 64.1 us
    pallas_call x1, Pallas kernels: 75.6 us -> 64.1 us  [local(): pl.pallas_call(functools.partial(kernel, n_rows, n_pair, plan), out_shape...]
where the time goes in v2:
time: 66.7 us; the launch traced here: 66.6 us
  Pallas kernels  64.1 us (96%)
  local copies, waits for them, and re-layouts  2.48 us (4%)
    pallas_call x1, Pallas kernels, local(): pl.pallas_call(functools.partial(kernel, n_rows, n_pair, plan), out_shape...  64.1 us
    unnamed x4, local copies, waits for them, and re-layouts  2.48 us

profile of v2, /device:TPU:1, one launch (start us, length us, event | category | flops | bytes accessed | tf_op | source)
XLA Modules:
  0.0 66.6 jit_solution(680377814271343507)
XLA Ops:
  0.0 0.7 %copy.3.side = s32[2,1]{1,0:T(2,128)S(1)} copy(s32[2,1]{0,1:T(1,128)} %param.3) | data formatting | bytes 16 | tf_op args[1]
  0.7 0.0 copy-start
  0.7 1.0 %copy-done = f32[192,512]{1,0:T(8,128)S(1)} copy-done((f32[192,512]{1,0:T(8,128)S(1)}, f32[192,512]{1,0:T(8,128)}, u32[]{:S(2)}) %copy-start) | copy-done | bytes 393240
  1.7 64.1 %shard_map.28 = f32[192,512]{1,0:T(8,128)S(1)} custom-call(s32[2,1]{1,0:T(2,128)S(1)} %copy.3.side, f32[192,512]{1,0:T(8,128)S(1)} %copy-done), custom_call_target="tpu_custom_call" | custom-call | tf_op jit(solution)/shard_map/pallas_call | solution.py:271
  65.8 0.7 %copy.5 = f32[192,512]{1,0:T(8,128)} copy(f32[192,512]{1,0:T(8,128)S(1)} %shard_map.28) | data formatting | bytes 786432
Async XLA Ops:
  0.7 1.0 %copy-start = (f32[192,512]{1,0:T(8,128)S(1)}, f32[192,512]{1,0:T(8,128)}, u32[]{:S(2)}) copy-start(f32[192,512]{1,0:T(8,128)} %x.1) | copy-start | bytes 1179652

commit v3 on v2

--- a/solution.py
+++ b/solution.py
@@ -11,7 +11,7 @@
 EPS = 1e-06
 TILE = 128
 PARTS = 4
-FAR = (0, 2)
+FAR = (1, 3)
 MESH = pl.DeviceIdType.MESH
 F32 = jnp.float32
 BF16 = jnp.bfloat16
@@ -33,8 +33,14 @@
     return both[:rows] + both[rows:] + dot(a[0], b[1])
 
 
-def off_diagonal(count):
-    return [(i, j) for i in range(count) for j in range(i + 1, count)]
+def layout(count):
+    mid = count // 2
+
+    def inner(low, high):
+        return ([(i, j) for i in range(low, high) for j in range(i + 1, high)]
+                + [(i, i) for i in range(low, high, 2)])
+
+    return inner(0, mid) + [(i, j) for i in range(mid) for j in range(mid, count)] + inner(mid, count)
 
 
 def packed_rows(width, unit):
@@ -48,51 +54,60 @@
             lax.broadcasted_iota(jnp.int32, (TILE, TILE), 1))
 
 
-def gram_pieces(left, right, acc):
-    high, low = split(jnp.concatenate([left, right], axis=1))
-    lhs = jnp.concatenate([high, high, low], axis=0).T
-    rhs = jnp.concatenate([high, low, high], axis=0)
-    count = rhs.shape[1] // TILE
+def gram_pieces(near, far, count, length):
+    mid = count // 2
     row, col = square_index()
-    strips = {}
+    sides, strips = {}, {}
+
+    def side(which):
+        if which not in sides:
+            high, low = split((far if which else near)())
+            sides[which] = (jnp.concatenate([high, high, low], axis=0).T,
+                            jnp.concatenate([high, low, high], axis=0))
+        return sides[which]
 
     def tile(i, j):
-        if i not in strips:
-            strips[i] = dot(lhs[i * TILE:(i + 1) * TILE], rhs[:, i * TILE:])
-        return strips[i][:, (j - i) * TILE:(j - i + 1) * TILE]
+        here, there = i // mid, j // mid
+        first = i % mid if here == there else 0
+        if (i, there) not in strips:
+            lhs = side(here)[0][i % mid * TILE:(i % mid + 1) * TILE]
+            strips[i, there] = dot(lhs, side(there)[1][:, first * TILE:])
+        at = (j % mid - first) * TILE
+        return strips[i, there][:, at:at + TILE]
 
     place = 0
-    for i, j in off_diagonal(count):
-        yield place, tile(i, j)
-        place += TILE
     tails = []
-    for i in range(0, count, 2):
-        later = tile(i + 1, i + 1)
-        tails.append(jnp.sum(jnp.where(row == col, later, 0.0), axis=0, keepdims=True))
-        yield place, jnp.where(row <= col, tile(i, i), later)
+    for i, j in layout(count):
+        if i != j:
+            value = tile(i, j)
+        else:
+            later = tile(i + 1, i + 1)
+            tails.append(jnp.sum(jnp.where(row == col, later, 0.0), axis=0, keepdims=True))
+            value = jnp.where(row <= col, tile(i, i), later)
+        yield place, value
         place += TILE
     for tail in tails:
         yield place, jnp.broadcast_to(tail, (8, TILE))
         place += 8
-    if place < acc.shape[0]:
-        yield place, jnp.zeros((acc.shape[0] - place, TILE), F32)
+    if place < length:
+        yield place, jnp.zeros((length - place, TILE), F32)
 
 
 def unpacked(full, count):
     row, col = square_index()
     at, place = {}, 0
-    for pair in off_diagonal(count):
-        at[pair] = full[place:place + TILE, :]
+    tail = len(layout(count)) * TILE
+    for i, j in layout(count):
+        both = full[place:place + TILE, :]
         place += TILE
-    tail = place + count // 2 * TILE
-    for i in range(0, count, 2):
-        both = full[place:place + TILE, :]
-        flipped = both.T
-        diagonal = jnp.broadcast_to(full[tail:tail + 1, :], (TILE, TILE))
-        at[i, i] = jnp.where(row <= col, both, flipped)
-        at[i + 1, i + 1] = jnp.where(row > col, both, jnp.where(row == col, diagonal, flipped))
-        place += TILE
-        tail += 8
+        if i != j:
+            at[i, j] = both
+        else:
+            flipped = both.T
+            diagonal = jnp.broadcast_to(full[tail:tail + 1, :], (TILE, TILE))
+            at[i, i] = jnp.where(row <= col, both, flipped)
+            at[i + 1, i + 1] = jnp.where(row > col, both, jnp.where(row == col, diagonal, flipped))
+            tail += 8
     return at
 
 
@@ -199,7 +214,7 @@
     return 1.5 * y - 0.5 * b
 
 
-def kernel(n_rows, n_pair, plan, side, x, out, acc, full, rbuf, leave, land,
+def kernel(n_rows, n_pair, plan, side, held, out, acc, full, rbuf, leave, land,
            row_send, row_recv, pair_send, pair_recv):
     p = lax.axis_index("pair")
     r = lax.axis_index("rows")
@@ -211,34 +226,51 @@
         pl.semaphore_signal(barrier, inc=1, device_id={"rows": other}, device_id_type=MESH)
     for other in (after, before):
         pl.semaphore_signal(barrier, inc=1, device_id={"pair": other}, device_id_type=MESH)
-    half = x.shape[1] // 2
+    rows, width = held.shape
+    half = width // 2
+    count = width // TILE
+    near = 1 - lax.rem(p, 2)
     pl.semaphore_wait(barrier, len(plan[0][2]) + 2)
     waits = []
+    arrived = None
     for turn in range(ROUNDS):
-        if turn == 0:
-            halves = lambda: (x[:, :half], x[:, half:])
-        else:
-            halves = lambda: (land[turn - 1, 0], land[turn - 1, 1])
-        waits += all_reduce(plan, gram_pieces(*halves(), acc.at[turn]), acc.at[turn], full.at[turn], rbuf.at[turn],
+        def block(which, turn=turn, arrived=arrived):
+            if turn == 0:
+                return held[:, which * half:(which + 1) * half]
+            if which not in seen:
+                seen.append(which)
+                arrived(which).wait_recv()
+            return land[turn - 1, near + which * (1 - 2 * near)]
+
+        seen = []
+        pieces = gram_pieces(lambda: block(0), lambda: block(1), count, acc.shape[1])
+        waits += all_reduce(plan, pieces, acc.at[turn], full.at[turn], rbuf.at[turn],
                             row_send.at[turn], row_recv.at[turn])
-        y = rotate(*halves(), full.at[turn], x.shape[0] * n_rows)
-        first, second = y[:, :half], y[:, half:]
-        chosen = jnp.full(first.shape, side[turn, 0], jnp.int32) == 0
-        leave[turn, 0] = jnp.where(chosen, first, second)
-        leave[turn, 1] = jnp.where(chosen, second, first)
-        sent = []
-        for way, other in enumerate((after, before)):
-            copy = pltpu.make_async_remote_copy(
+        y = rotate(block(0), block(1), full.at[turn], rows * n_rows)
+        one, two = y[:, :half], y[:, half:]
+        flip = near if turn else 0
+        chosen = jnp.broadcast_to(side[0:1, turn:turn + 1], one.shape)
+        forward = jnp.where(chosen == 0, 0, 1) == flip
+        leave[turn, 0] = jnp.where(forward, one, two)
+        leave[turn, 1] = jnp.where(forward, two, one)
+
+        def remote(way, other, turn=turn):
+            return pltpu.make_async_remote_copy(
                 src_ref=leave.at[turn, way], dst_ref=land.at[turn, way],
                 send_sem=pair_send.at[turn, way], recv_sem=pair_recv.at[turn, way],
                 device_id={"pair": other}, device_id_type=MESH)
+
+        sent = [remote(way, other) for way, other in enumerate((after, before))]
+        for copy in sent:
             copy.start()
-            sent.append(copy)
-        for copy in sent:
-            copy.wait_recv()
         waits += sent
-    out[:, :half] = land[ROUNDS - 1, 0]
-    out[:, half:] = land[ROUNDS - 1, 1]
+
+        def arrived(which, remote=remote):
+            return remote(near + which * (1 - 2 * near), after)
+
+    for way, copy in enumerate(sent):
+        copy.wait_recv()
+        out[:, way * half:(way + 1) * half] = land[ROUNDS - 1, way]
     for copy in waits:
         copy.wait_send()
 
@@ -271,7 +303,7 @@
         return pl.pallas_call(
             functools.partial(kernel, n_rows, n_pair, plan),
             out_shape=jax.ShapeDtypeStruct((rows, width), F32),
-            in_specs=[pl.BlockSpec(memory_space=pltpu.SMEM), vmem],
+            in_specs=[vmem, vmem],
             out_specs=vmem,
             scratch_shapes=[
                 pltpu.VMEM((ROUNDS, gram_rows, TILE), F32),
@@ -286,7 +318,7 @@
             ],
             compiler_params=pltpu.CompilerParams(
                 collective_id=0, has_side_effects=True, vmem_limit_bytes=48 << 20),
-        )(keep_side, snapshot)
+        )(keep_side.T, snapshot)
 
     placed = (P("rows", "pair"), P(None, "pair"))
     return jax.shard_map(

time: 66.7 us -> 64.2 us (0.963)
  Pallas kernels: 64.1 us -> 61.6 us
    pallas_call x1, Pallas kernels: 64.1 us -> 61.6 us  [local(): pl.pallas_call(functools.partial(kernel, n_rows, n_pair, plan), out_shape...]
    unnamed x4 -> x5, local copies, waits for them, and re-layouts: 2.48 us -> 2.4 us
where the time goes in v3:
time: 64.2 us; the launch traced here: 64 us
  Pallas kernels  61.6 us (96%)
  local copies, waits for them, and re-layouts  2.4 us (4%)
    pallas_call x1, Pallas kernels, local(): pl.pallas_call(functools.partial(kernel, n_rows, n_pair, plan), out_shape...  61.6 us
    unnamed x5, local copies, waits for them, and re-layouts  2.4 us

profile of v3, /device:TPU:1, one launch (start us, length us, event | category | flops | bytes accessed | tf_op | source)
XLA Modules:
  0.0 64.0 jit_solution(13202952888996244606)
XLA Ops:
  0.0 0.0 copy-start.1
  0.0 0.7 %copy-done.1 = s32[2,1]{0,1:T(1,128)S(1)} copy-done((s32[2,1]{0,1:T(1,128)S(1)}, s32[2,1]{0,1:T(1,128)}, u32[]{:S(2)}) %copy-start.1) | copy-done | bytes 32
  0.7 0.0 copy-start
  0.7 1.0 %copy-done = f32[192,512]{1,0:T(8,128)S(1)} copy-done((f32[192,512]{1,0:T(8,128)S(1)}, f32[192,512]{1,0:T(8,128)}, u32[]{:S(2)}) %copy-start) | copy-done | bytes 393240
  1.7 61.6 %shard_map.28 = f32[192,512]{1,0:T(8,128)S(1)} custom-call(s32[1,2]{1,0:T(1,128)S(1)} %bitcast.1, f32[192,512]{1,0:T(8,128)S(1)} %copy-done), custom_call_target="tpu_custom_call" | custom-call | tf_op jit(solution)/shard_map/pallas_call | solution.py:303
  63.3 0.7 %copy.4 = f32[192,512]{1,0:T(8,128)} copy(f32[192,512]{1,0:T(8,128)S(1)} %shard_map.28) | data formatting | bytes 786432
Async XLA Ops:
  0.0 0.7 %copy-start.1 = (s32[2,1]{0,1:T(1,128)S(1)}, s32[2,1]{0,1:T(1,128)}, u32[]{:S(2)}) copy-start(s32[2,1]{0,1:T(1,128)} %param.3) | copy-start | bytes 28
  0.7 1.0 %copy-start = (f32[192,512]{1,0:T(8,128)S(1)}, f32[192,512]{1,0:T(8,128)}, u32[]{:S(2)}) copy-start(f32[192,512]{1,0:T(8,128)} %held.1) | copy-start | bytes 1179652

commit v4 on v3

--- a/solution.py
+++ b/solution.py
@@ -31,6 +31,13 @@
     rows = a[0].shape[0]
     both = dot(jnp.concatenate([a[0], a[1]], axis=0), b[0])
     return both[:rows] + both[rows:] + dot(a[0], b[1])
+
+
+def dot_symmetric(a, b):
+    mid = a[0].shape[0] // 2
+    top = dot_split((a[0][:mid], a[1][:mid]), b)
+    low = dot_split((a[0][mid:], a[1][mid:]), (b[0][:, mid:], b[1][:, mid:]))
+    return jnp.concatenate([top, jnp.concatenate([top[:, mid:].T, low], axis=1)], axis=0)
 
 
 def layout(count):
@@ -198,8 +205,8 @@
     e_mat = jnp.concatenate(
         [jnp.concatenate([at[i, j] for j in range(count)], axis=1) for i in range(count)], axis=0)
     e_half = split(e_mat)
-    e_two = dot_split(e_half, e_half)
-    e_three = dot_split(e_half, split(e_two))
+    e_two = dot_symmetric(e_half, e_half)
+    e_three = dot_symmetric(e_half, split(e_two))
     wide = (lax.broadcasted_iota(jnp.int32, (width, width), 0)
             == lax.broadcasted_iota(jnp.int32, (width, width), 1))
     b_one = (9.0 * e_mat - 6.0 * e_two + e_three) * 0.25

time: 64.2 us -> 63.4 us (0.988)
  Pallas kernels: 61.6 us -> 60.7 us
    pallas_call x1, Pallas kernels: 61.6 us -> 60.7 us  [local(): pl.pallas_call(functools.partial(kernel, n_rows, n_pair, plan), out_shape...]
where the time goes in v4:
time: 63.4 us; the launch traced here: 63.1 us
  Pallas kernels  60.7 us (96%)
  local copies, waits for them, and re-layouts  2.4 us (4%)
    pallas_call x1, Pallas kernels, local(): pl.pallas_call(functools.partial(kernel, n_rows, n_pair, plan), out_shape...  60.7 us
    unnamed x5, local copies, waits for them, and re-layouts  2.4 us

profile of v4, /device:TPU:1, one launch (start us, length us, event | category | flops | bytes accessed | tf_op | source)
XLA Modules:
  0.0 63.1 jit_solution(8045382498822551370)
XLA Ops:
  0.0 0.0 copy-start.1
  0.0 0.7 %copy-done.1 = s32[2,1]{0,1:T(1,128)S(1)} copy-done((s32[2,1]{0,1:T(1,128)S(1)}, s32[2,1]{0,1:T(1,128)}, u32[]{:S(2)}) %copy-start.1) | copy-done | bytes 32
  0.7 0.0 copy-start
  0.7 1.0 %copy-done = f32[192,512]{1,0:T(8,128)S(1)} copy-done((f32[192,512]{1,0:T(8,128)S(1)}, f32[192,512]{1,0:T(8,128)}, u32[]{:S(2)}) %copy-start) | copy-done | bytes 393240
  1.7 60.7 %shard_map.28 = f32[192,512]{1,0:T(8,128)S(1)} custom-call(s32[1,2]{1,0:T(1,128)S(1)} %bitcast.1, f32[192,512]{1,0:T(8,128)S(1)} %copy-done), custom_call_target="tpu_custom_call" | custom-call | tf_op jit(solution)/shard_map/pallas_call | solution.py:310
  62.4 0.7 %copy.4 = f32[192,512]{1,0:T(8,128)} copy(f32[192,512]{1,0:T(8,128)S(1)} %shard_map.28) | data formatting | bytes 786432
Async XLA Ops:
  0.0 0.7 %copy-start.1 = (s32[2,1]{0,1:T(1,128)S(1)}, s32[2,1]{0,1:T(1,128)}, u32[]{:S(2)}) copy-start(s32[2,1]{0,1:T(1,128)} %param.3) | copy-start | bytes 28
  0.7 1.0 %copy-start = (f32[192,512]{1,0:T(8,128)S(1)}, f32[192,512]{1,0:T(8,128)}, u32[]{:S(2)}) copy-start(f32[192,512]{1,0:T(8,128)} %held.1) | copy-start | bytes 1179652
